TPU v7x, 32 devices: a whole 2x2x4 slice. The times are simulated.
32 devices in a mesh: seq: 8 (over y, x, core), dp: 4 (over z).
Axes of the slice: x: 2, y: 2, z: 4, core: 2. Of those that a mesh axis runs over, the one named last changes fastest.
Arguments:
- history: bfloat16 [9, 1024, 4096], P(None, 'seq', 'dp'), may hold values from -6 to 6
- cotangent: bfloat16 [1024, 4096], P('seq', 'dp'), may hold values from -6 to 6
- bucket_len: int32 [4, 8, 2], P('dp', 'seq'), may hold values from 32 to 96, as said below
- valid_len: int32 [4, 8, 2], P('dp', 'seq'), may hold values from 1 to 96, as said below
- gen_gain: float32 [1024], replicated, may hold values from 0.25 to 1.75
- gen_in: bfloat16 [1024, 40], replicated, may hold values from -0.1875 to 0.1875
- gen_out: float32 [40, 4, 9], replicated, may hold values from -1 to 1
- gen_bias: float32 [4, 9], replicated, may hold values from -3 to 3
- norm_gain: float32 [2, 1024], replicated, may hold values from 0.25 to 1.75
- norm_bias: float32 [2, 1024], replicated, may hold values from -2 to 2
- w_in: bfloat16 [1024, 7, 1024], P('seq'), may hold values from -0.1875 to 0.1875
- in_bias: float32 [7, 1024], replicated, may hold values from -2 to 2
- w_out: bfloat16 [1024, 1024], P('seq'), may hold values from -0.75 to 0.75
- w_down: bfloat16 [1024, 4096], P('seq'), may hold values from -0.09375 to 0.09375
- out_bias: float32 [1024], replicated, may hold values from -2 to 2
Outputs:
- new_state: bfloat16 [1024, 4096], P('seq', 'dp')
- history_grad: bfloat16 [9, 1024, 4096], P(None, 'seq', 'dp')
- mix_mean: float32 [4, 9], replicated
- mix_var: float32 [4, 9], replicated
- gen_gain_grad: float32 [1024], replicated
- gen_in_grad: float32 [1024, 40], replicated
- gen_out_grad: float32 [40, 4, 9], replicated
- gen_bias_grad: float32 [4, 9], replicated
- norm_gain_grad: float32 [2, 1024], replicated
- norm_bias_grad: float32 [2, 1024], replicated
- w_in_grad: float32 [1024, 7, 1024], P('seq')
- in_bias_grad: float32 [7, 1024], replicated
- w_out_grad: float32 [1024, 1024], P('seq')
- w_down_grad: float32 [1024, 4096], P('seq')
- out_bias_grad: float32 [1024], replicated
Inputs may be any that keep to these rules, and one draw needn't show every extreme that they name: `bucket_len`: the two buckets of one token block together hold 128 tokens. Each bucket's valid tokens are its first valid_len tokens, at least one and at most the bucket's length.
All inputs are finite; a program needn't handle non-finite values.
Results may differ from a plain program's by a relative error of at most 0.015.
Values may be sent and summed in bfloat16 or wider, within the bound.
A program may use at most 256 MiB of HBM per device.

v0:
```python
import math
import jax
import jax.numpy as jnp
from jax import lax
from jax.sharding import PartitionSpec as P

HEADS = 16
HEAD_DIM = 64
ROT = 16
ln_eps = 1e-05
rms_eps = 1e-06
masked_score = -1e30
highest = lax.Precision.HIGHEST


def gelu_exact(values):
    return jax.nn.gelu(values, approximate=False)


def rotary_tables(position):
    freq_index = jnp.arange(ROT // 2, dtype=jnp.float32)
    inverse_freq = jnp.exp(freq_index * (-2.0 * math.log(10000.0) / ROT))
    angles = position.astype(jnp.float32)[:, None] * inverse_freq[None, :]
    return (jnp.cos(angles), jnp.sin(angles))


def rotate(values, cosine, sine):
    half = ROT // 2
    former = values[..., :half]
    latter = values[..., half:ROT]
    cos_heads = cosine[:, None, :]
    sin_heads = sine[:, None, :]
    return jnp.concatenate(
        [
            former * cos_heads - latter * sin_heads,
            latter * cos_heads + former * sin_heads,
            values[..., ROT:],
        ],
        axis=-1,
    )


def token_layout(lengths, counts, tokens):
    index = jnp.arange(tokens, dtype=jnp.int32)
    second = index >= lengths[0]
    position = index - jnp.where(second, lengths[0], 0)
    valid = position < jnp.where(second, counts[1], counts[0])
    return (second, position, valid)


def normalize(streams):
    centre = jnp.mean(streams, axis=-1, keepdims=True)
    centred = streams - centre
    inverse = lax.rsqrt(jnp.mean(centred * centred, axis=-1, keepdims=True) + ln_eps)
    return (centred * inverse, inverse)


def normalize_back(grad_scaled, scaled, inverse):
    mean_grad = jnp.mean(grad_scaled, axis=-1, keepdims=True)
    mean_along = jnp.mean(grad_scaled * scaled, axis=-1, keepdims=True)
    return inverse * (grad_scaled - mean_grad - scaled * mean_along)


def per_device(
    history,
    cotangent,
    bucket_len,
    valid_len,
    gen_gain,
    gen_in,
    gen_out,
    gen_bias,
    norm_gain,
    norm_bias,
    w_in,
    in_bias,
    w_out,
    w_down,
    out_bias,
):
    states = history.shape[0]
    stacked = jnp.concatenate([history, cotangent[None]], axis=0)
    arrived = lax.all_to_all(stacked, "seq", split_axis=2, concat_axis=1, tiled=True)
    arrived_rows = jnp.swapaxes(arrived, 1, 2)
    hist_local = arrived_rows[:states]
    cot_local = arrived_rows[states]
    tokens = hist_local.shape[1]
    width = hist_local.shape[2]
    second, position, valid = token_layout(bucket_len.reshape(2), valid_len.reshape(2), tokens)
    valid_float = valid.astype(jnp.float32)
    last = hist_local[states - 1].astype(jnp.float32)
    rms = lax.rsqrt(jnp.mean(last * last, axis=-1, keepdims=True) + rms_eps)
    gen_normed = (last * rms * gen_gain).astype(jnp.bfloat16)
    gen_pre = jnp.dot(gen_normed, gen_in, preferred_element_type=jnp.float32)
    gen_hidden, gen_pull = jax.vjp(gelu_exact, gen_pre)
    mixing = jnp.einsum("th,hsj->tsj", gen_hidden, gen_out, precision=highest) + gen_bias
    weighted = mixing * valid_float[:, None, None]
    stat_sums = jnp.sum(weighted, axis=0)
    stat_squares = jnp.sum(weighted * mixing, axis=0)
    stat_count = jnp.sum(valid_float)
    streams = mixing[:, :, 0].T[:, :, None] * hist_local[0]
    for state in range(1, states):
        streams = streams + mixing[:, :, state].T[:, :, None] * hist_local[state]
    scaled, inverse = normalize(streams)
    normed_attn = (scaled[:3] * norm_gain[0] + norm_bias[0]).astype(jnp.bfloat16)
    normed_mlp = (scaled[3] * norm_gain[1] + norm_bias[1]).astype(jnp.bfloat16)
    piece = lax.all_gather(w_in, "seq", axis=0, tiled=True)
    attn_part = jnp.einsum(
        "stk,nsk->stn", normed_attn, piece[:, :3], preferred_element_type=jnp.float32
    )
    mlp_part = jnp.einsum(
        "tk,njk->jtn", normed_mlp, piece[:, 3:], preferred_element_type=jnp.float32
    )
    projected = jnp.concatenate([attn_part, mlp_part], axis=0) + in_bias[:, None, :]
    cosine, sine = rotary_tables(position)
    heads_shape = (tokens, HEADS, HEAD_DIM)
    queries = (rotate(projected[0].reshape(heads_shape), cosine, sine) * HEAD_DIM ** (-0.5)).astype(
        jnp.bfloat16
    )
    keys = rotate(projected[1].reshape(heads_shape), cosine, sine).astype(jnp.bfloat16)
    values = projected[2].reshape(heads_shape).astype(jnp.bfloat16)
    index = jnp.arange(tokens, dtype=jnp.int32)
    allowed = (
        (second[:, None] == second[None, :]) & (index[None, :] <= index[:, None]) & valid[None, :]
    )
    scores = jnp.einsum("qhd,khd->hqk", queries, keys, preferred_element_type=jnp.float32)
    scores = jnp.where(allowed[None], scores, masked_score)
    top = jnp.max(scores, axis=-1, keepdims=True)
    weights = jnp.exp(scores - top)
    weight_total = jnp.sum(weights, axis=-1, keepdims=True)
    log_total = top + jnp.log(weight_total)
    probs_low = (weights / weight_total).astype(jnp.bfloat16)
    attended = jnp.einsum("hqk,khd->qhd", probs_low, values, preferred_element_type=jnp.float32)
    attn_low = attended.reshape(tokens, width).astype(jnp.bfloat16)
    gelu_up, up_pull = jax.vjp(gelu_exact, projected[3:])
    gelu_low = gelu_up.astype(jnp.bfloat16)
    grad_out_low = jnp.where(valid[:, None], cot_local, jnp.zeros_like(cot_local))
    piece_out, piece_down = lax.all_gather((w_out, w_down), "seq", axis=0, tiled=True)
    down_part = piece_down.reshape(piece_down.shape[0], 4, width)
    result = jnp.einsum("tk,nk->tn", attn_low, piece_out, preferred_element_type=jnp.float32)
    branch = result + jnp.einsum(
        "jtk,njk->tn", gelu_low, down_part, preferred_element_type=jnp.float32
    )
    new_local = (streams[3] + branch + out_bias).astype(jnp.bfloat16)
    piece_out = lax.all_gather(w_out, "seq", axis=0, tiled=True)
    piece_down = lax.all_gather(w_down, "seq", axis=0, tiled=True)
    count = piece_out.shape[0]
    part = grad_out_low
    attn_add = jnp.einsum("tn,nk->tk", part, piece_out, preferred_element_type=jnp.float32)
    gelu_add = jnp.einsum(
        "tn,njk->jtk", part, piece_down.reshape(count, 4, width), preferred_element_type=jnp.float32
    )
    grad_attn = attn_add
    part = grad_out_low
    term_out = jnp.einsum("tn,tk->nk", part, attn_low, preferred_element_type=jnp.float32)
    term_down = jnp.einsum(
        "tn,jtk->njk", part, gelu_low, preferred_element_type=jnp.float32
    ).reshape(lax.axis_size("seq") * w_out.shape[0], 4 * width)
    out_grads = lax.psum_scatter(
        jnp.concatenate([term_out, term_down], axis=1).astype(jnp.bfloat16),
        "seq",
        scatter_dimension=0,
        tiled=True,
    )
    out_bias_grad = jnp.sum(grad_out_low.astype(jnp.float32), axis=0)
    grad_attended = grad_attn.astype(jnp.bfloat16).reshape(heads_shape)
    rescored = jnp.einsum("qhd,khd->hqk", queries, keys, preferred_element_type=jnp.float32)
    probs = jnp.where(allowed[None], jnp.exp(rescored - log_total), 0.0)
    grad_values = jnp.einsum(
        "hqk,qhd->khd",
        probs.astype(jnp.bfloat16),
        grad_attended,
        preferred_element_type=jnp.float32,
    )
    grad_probs = jnp.einsum(
        "qhd,khd->hqk", grad_attended, values, preferred_element_type=jnp.float32
    )
    grad_scores = (
        probs * (grad_probs - jnp.sum(probs * grad_probs, axis=-1, keepdims=True))
    ).astype(jnp.bfloat16)
    grad_queries = jnp.einsum(
        "hqk,khd->qhd", grad_scores, keys, preferred_element_type=jnp.float32
    ) * HEAD_DIM ** (-0.5)
    grad_keys = jnp.einsum("hqk,qhd->khd", grad_scores, queries, preferred_element_type=jnp.float32)
    grad_up = up_pull(gelu_add)[0]
    grad_proj = jnp.concatenate(
        [
            rotate(grad_queries, cosine, -sine).reshape(1, tokens, width),
            rotate(grad_keys, cosine, -sine).reshape(1, tokens, width),
            grad_values.reshape(1, tokens, width),
            grad_up,
        ],
        axis=0,
    )
    in_bias_grad = jnp.sum(grad_proj, axis=1)
    grad_proj_low = grad_proj.astype(jnp.bfloat16)
    piece = lax.all_gather(w_in, "seq", axis=0, tiled=True)
    part = grad_proj_low
    attn_add = jnp.einsum(
        "stn,nsk->stk", part[:3], piece[:, :3], preferred_element_type=jnp.float32
    )
    mlp_add = jnp.einsum("jtn,njk->tk", part[3:], piece[:, 3:], preferred_element_type=jnp.float32)
    part = grad_proj_low
    attn_term = jnp.einsum(
        "stn,stk->nsk", part[:3], normed_attn, preferred_element_type=jnp.float32
    )
    mlp_term = jnp.einsum("jtn,tk->njk", part[3:], normed_mlp, preferred_element_type=jnp.float32)
    in_grads = lax.psum_scatter(
        jnp.concatenate([attn_term, mlp_term], axis=1).astype(jnp.bfloat16),
        "seq",
        scatter_dimension=0,
        tiled=True,
    )
    norm_gain_grad = jnp.stack(
        [jnp.sum(attn_add * scaled[:3], axis=(0, 1)), jnp.sum(mlp_add * scaled[3], axis=0)]
    )
    norm_bias_grad = jnp.stack([jnp.sum(attn_add, axis=(0, 1)), jnp.sum(mlp_add, axis=0)])
    grad_attn_streams = normalize_back(attn_add * norm_gain[0], scaled[:3], inverse[:3])
    grad_mlp_stream = normalize_back(
        mlp_add * norm_gain[1], scaled[3], inverse[3]
    ) + grad_out_low.astype(jnp.float32)
    grad_streams = jnp.concatenate([grad_attn_streams, grad_mlp_stream[None]], axis=0)
    grad_mixing = jnp.stack(
        [
            jnp.einsum(
                "std,td->ts", grad_streams, hist_local[state].astype(jnp.float32), precision=highest
            )
            for state in range(states)
        ],
        axis=-1,
    )
    hist_terms = [
        jnp.einsum("ts,std->td", mixing[:, :, state], grad_streams, precision=highest)
        for state in range(states)
    ]
    gen_bias_grad = jnp.sum(grad_mixing, axis=0)
    gen_out_grad = jnp.einsum("th,tsj->hsj", gen_hidden, grad_mixing, precision=highest)
    grad_hidden = jnp.einsum("tsj,hsj->th", grad_mixing, gen_out, precision=highest)
    grad_pre_low = gen_pull(grad_hidden)[0].astype(jnp.bfloat16)
    gen_in_grad = jnp.einsum(
        "tk,th->kh", gen_normed, grad_pre_low, preferred_element_type=jnp.float32
    )
    grad_gen = jnp.einsum("th,kh->tk", grad_pre_low, gen_in, preferred_element_type=jnp.float32)
    gen_gain_grad = jnp.sum(grad_gen * last * rms, axis=0)
    gained = grad_gen * gen_gain
    grad_last = rms * gained - last * (rms * rms * rms) * jnp.mean(
        gained * last, axis=-1, keepdims=True
    )
    hist_stack = jnp.stack(hist_terms[: states - 1] + [hist_terms[states - 1] + grad_last]).astype(
        jnp.bfloat16
    )
    departing = jnp.swapaxes(jnp.concatenate([new_local[None], hist_stack], axis=0), 1, 2)
    returned = lax.all_to_all(departing, "seq", split_axis=1, concat_axis=2, tiled=True)
    w_in_grad, out_total = (
        lax.psum(in_grads, "dp").astype(jnp.float32),
        lax.psum(out_grads, "dp").astype(jnp.float32),
    )
    w_out_grad = out_total[:, :width]
    w_down_grad = out_total[:, width:]
    joined = lax.psum(
        (
            gen_gain_grad,
            gen_in_grad,
            gen_out_grad,
            gen_bias_grad,
            norm_gain_grad,
            norm_bias_grad,
            in_bias_grad,
            out_bias_grad,
            stat_sums,
            stat_squares,
            stat_count,
        ),
        ("seq", "dp"),
    )
    small_totals = joined[:8]
    stat_totals = joined[8:]
    mix_mean = stat_totals[0] / stat_totals[2]
    mix_var = stat_totals[1] / stat_totals[2] - mix_mean * mix_mean
    return (
        returned[0],
        returned[1:],
        mix_mean,
        mix_var,
        small_totals[0],
        small_totals[1],
        small_totals[2],
        small_totals[3],
        small_totals[4],
        small_totals[5],
        w_in_grad,
        small_totals[6],
        w_out_grad,
        w_down_grad,
        small_totals[7],
    )


def solution(mesh):
    in_specs = (
        P(None, "seq", "dp"),
        P("seq", "dp"),
        P("dp", "seq", None),
        P("dp", "seq", None),
        P(),
        P(),
        P(),
        P(),
        P(),
        P(),
        P("seq", None, None),
        P(),
        P("seq", None),
        P("seq", None),
        P(),
    )
    out_specs = (
        P("seq", "dp"),
        P(None, "seq", "dp"),
        P(),
        P(),
        P(),
        P(),
        P(),
        P(),
        P(),
        P(),
        P("seq", None, None),
        P(),
        P("seq", None),
        P("seq", None),
        P(),
    )
    return jax.shard_map(
        per_device, mesh=mesh, in_specs=in_specs, out_specs=out_specs, check_vma=False
    )
```

profile of v0, /device:TPU:8, one launch (start us, length us, event | category | flops | bytes accessed | tf_op | source)
XLA Modules:
  0.0 705.1 jit_solution(17909491425658481265)
XLA Ops:
  11.4 7.4 %copy.110 = bf16[9,128,1024]{1,0,2:T(8,128)(2,1)} copy(bf16[9,128,1024]{2,1,0:T(8,128)(2,1)S(1)} %copy-done.17) | data formatting | bytes 4718592 | tf_op args[0]
  18.8 6.1 pad_maximum_fusion.2
  24.9 4.7 all-to-all-start
  33.1 64.4 %all-to-all-done = bf16[10,128,1024]{1,0,2:T(8,128)(2,1)} async-done(((bf16[10,128,1024]{1,0,2:T(8,128)(2,1)}), bf16[10,128,1024]{1,0,2:T(8,128)(2,1)}, u32[]{:S(2)}, u32[]{:S(2)}) %all-to-all-start) | async-done | bytes 2621472 | tf_op jit(solution)/shard_map/all_to_all | solution.py:83
  97.5 5.4 copy.298
  117.8 33.5 %all-gather.4.cloned.1.call-done = bf16[1024,7,1024]{2,0,1:T(8,128)(2,1)} async-done(((bf16[128,7,1024]{2,0,1:T(8,128)(2,1)}), bf16[1024,7,1024]{2,0,1:T(8,128)(2,1)}) %all-gather.4.cloned.1.call-update) | async-done | bytes 14680080 | tf_op jit(solution)/shard_map/all_gather | solution.py:107
  151.3 5.0 fusion.6
  156.3 6.3 fusion.22
  184.9 7.3 %multiply_convert_fusion = (bf16[4,128,1024]{2,1,0:T(8,128)(2,1)}, f32[4,128,1024]{2,1,0:T(8,128)}) fusion(f32[7,128,1024]{2,1,0:T(8,128)} %copy-done.3), kind=kLoop, calls=%fused_computation.30 | loop fusion | flops 34078720 | bytes 5242880 | tf_op jit(solution)/shard_map/convert_element_type | solution.py:136
  192.2 16.9 %all-gather.8.cloned.1.call-done = bf16[1024,4096]{0,1:T(8,128)(2,1)} async-done(((bf16[128,4096]{0,1:T(8,128)(2,1)}), bf16[1024,4096]{0,1:T(8,128)(2,1)}) %all-gather.8.cloned.1.call-update) | async-done | bytes 8388624 | tf_op jit(solution)/shard_map/all_gather | solution.py:138
  209.1 8.0 %fusion.15 = f32[4,128,1024]{2,1,0:T(8,128)S(1)} fusion(f32[4,128,1024]{2,1,0:T(8,128)} %get-tuple-element.106, f32[7,128,1024]{2,1,0:T(8,128)} %copy-done.3, bf16[1024,4,1024]{0,2,1:T(8,128)(2,1)} %bitcast.374, pred[128]{0:T(512)(128)(4,1)S(1)} %copy-done.57, bf16[10,128,1024]{2,1,0:T(8,128)(2,1)} %bitcast.365), kind=kOutput, calls=%fused_computation.28 | convolution fusion | flops 1080688640 | bytes 14942336 | tf_op jit(solution)/shard_map/tn,njk->jtk/dot_general | solution.py:150
  223.3 8.3 %pad_maximum_fusion = bf16[1024,7,1024]{0,2,1:T(8,128)(2,1)} fusion(bf16[1024,4,1024]{0,2,1:T(8,128)(2,1)S(1)} %convert_bitcast_fusion, bf16[1024,3,1024]{0,2,1:T(8,128)(2,1)S(1)} %convert_bitcast_fusion.1), kind=kLoop, calls=%fused_computation | loop fusion | flops 7340032 | bytes 29360128 | tf_op jit(solution)/shard_map/concatenate | solution.py:209
  231.6 18.5 %copy.186 = bf16[1024,7168]{1,0:T(8,128)(2,1)} copy(bf16[1024,7168]{0,1:T(8,128)(2,1)} %bitcast.360) | data formatting | bytes 29360128
  264.6 6.3 pad_maximum_fusion.1
  278.1 5.9 multiply_reduce_fusion.5
  284.0 5.0 multiply_reduce_fusion.1
  291.5 4.8 fusion.68
  296.3 4.8 fusion.66
  301.2 5.0 fusion.64
  306.3 4.8 fusion.62
  311.8 4.8 fusion.60
  317.2 5.2 fusion.58
  323.1 4.8 fusion.56
  328.5 4.8 fusion.54
  333.9 5.6 fusion.52
  343.5 5.2 fusion.154
  348.8 4.9 convolution_bitcast_fusion.1
  388.6 51.7 %reduce-scatter.5.cloned.1.call-done = bf16[128,5120]{1,0:T(8,128)(2,1)} async-done(((bf16[1024,5120]{1,0:T(8,128)(2,1)}), bf16[128,5120]{1,0:T(8,128)(2,1)}) %reduce-scatter.5.cloned.1.call-update) | async-done | bytes 1310736 | tf_op jit(solution)/shard_map/reduce_scatter | solution.py:159
  457.2 6.8 copy.129
  464.1 4.8 all-to-all-start.1
  472.8 81.4 %all-reduce = (f32[4,9]{1,0:T(4,128)S(1)}, f32[]{:T(128)}, f32[4,9]{1,0:T(4,128)S(1)}, f32[1024]{0:T(1024)}, f32[40,4,9]{0,2,1:T(8,128)S(1)}, /*index=5*/f32[4,9...) all-reduce(f32[4,9]{1,0:T(4,128)S(1)} %copy-done.85, ...), channel_id=1, replica_groups=mesh['seq'=8,'dp'=4] {'seq','dp'}, use_global_device_ids=true, to_apply=%region_12.13 | all-reduce | flops 14861 | bytes 118888 | tf_op jit(solution)/shard_map/psum | solution.py:260
  574.8 121.5 %all-reduce.5.cloned.1.call-done = f32[1024,40]{0,1:T(8,128)} async-done(((f32[1024,40]{0,1:T(8,128)}), f32[1024,40]{0,1:T(8,128)}) %all-reduce.5.cloned.1.call-update) | async-done | bytes 163856 | tf_op jit(solution)/shard_map/psum | solution.py:260
  (345 shorter events, 159.7 us)
Async XLA Ops:
  7.2 101.2 %copy-start = (bf16[1024,40]{0,1:T(8,128)(2,1)S(1)}, bf16[1024,40]{0,1:T(8,128)(2,1)}, u32[]{:S(2)}) copy-start(bf16[1024,40]{0,1:T(8,128)(2,1)} %param.20) | copy-start | bytes 245764
  7.2 108.2 %all-gather.6.cloned.1.call-start = ((), (), s32[]{:S(2)}) async-start(), calls=%async_computation.5 | async-start | bytes 2359296 | tf_op jit(solution)/shard_map/all_gather | solution.py:138
  7.9 143.4 %all-gather.4.cloned.1.call-start = ((), (), s32[]{:S(2)}) async-start(), calls=%async_computation.4 | async-start | bytes 16515072 | tf_op jit(solution)/shard_map/all_gather | solution.py:107
  8.7 200.4 %all-gather.8.cloned.1.call-start = ((), (), s32[]{:S(2)}) async-start(), calls=%async_computation.6 | async-start | bytes 9437184 | tf_op jit(solution)/shard_map/all_gather | solution.py:138
  24.9 8.1 %copy-start.86 = (f32[2,1024]{1,0:T(2,128)S(1)}, f32[2,1024]{1,0:T(2,128)}, u32[]{:S(2)}) copy-start(f32[2,1024]{1,0:T(2,128)} %param.24) | copy-start | bytes 24580
  24.9 8.1 %copy-start.87 = (f32[2,1024]{1,0:T(2,128)S(1)}, f32[2,1024]{1,0:T(2,128)}, u32[]{:S(2)}) copy-start(f32[2,1024]{1,0:T(2,128)} %param.23) | copy-start | bytes 24580
  24.9 72.6 %all-to-all-start = ((bf16[10,128,1024]{1,0,2:T(8,128)(2,1)}), bf16[10,128,1024]{1,0,2:T(8,128)(2,1)}, u32[]{:S(2)}, u32[]{:S(2)}) async-start(bf16[10,128,1024]{1,0,2:T(8,128)(2,1)} %pad_maximum_fusion.2), calls=%async_computation | async-start | bytes 8388608 | tf_op jit(solution)/shard_map/all_to_all | solution.py:83
  29.6 355.1 %reduce-scatter.7.cloned.1.call-start = ((), (), s32[]{:S(2)}) async-start(), calls=%async_computation.9 | async-start | bytes 16515072
  32.2 83.3 %copy-start.56 = (pred[128]{0:T(512)(128)(4,1)}, pred[128]{0:T(512)(128)(4,1)S(1)}, u32[]{:S(2)}) copy-start(pred[128]{0:T(512)(128)(4,1)S(1)} %get-tuple-element.104) | copy-start | bytes 388
  33.0 118.3 %copy-start.78 = (f32[1,1024]{1,0:T(1,128)}, f32[1,1024]{1,0:T(1,128)S(1)}, u32[]{:S(2)}) copy-start(f32[1,1024]{1,0:T(1,128)S(1)} %get-tuple-element.152) | copy-start | bytes 12292
  33.0 123.3 %copy-start.82 = (f32[1,1024]{1,0:T(1,128)}, f32[1,1024]{1,0:T(1,128)S(1)}, u32[]{:S(2)}) copy-start(f32[1,1024]{1,0:T(1,128)S(1)} %get-tuple-element.153) | copy-start | bytes 12292
  156.3 6.3 copy-start.53
  184.9 24.2 %copy-start.57 = (pred[128]{0:T(512)(128)(4,1)S(1)}, pred[128]{0:T(512)(128)(4,1)}, u32[]{:S(2)}) copy-start(pred[128]{0:T(512)(128)(4,1)} %copy-done.56) | copy-start | bytes 388
  209.1 9.3 %copy-start.11 = (f32[1,128,1024]{2,1,0:T(8,128)S(1)}, f32[1,128,1024]{2,1,0:T(8,128)}, u32[]{:S(2)}) copy-start(f32[1,128,1024]{2,1,0:T(8,128)} %copy.127) | copy-start | bytes 1572868
  209.1 9.3 %copy-start.13 = (f32[1,128,1024]{2,1,0:T(8,128)S(1)}, f32[1,128,1024]{2,1,0:T(8,128)}, u32[]{:S(2)}) copy-start(f32[1,128,1024]{2,1,0:T(8,128)} %copy.126) | copy-start | bytes 1572868
  209.1 9.3 %copy-start.15 = (f32[1,128,1024]{2,1,0:T(8,128)S(1)}, f32[1,128,1024]{2,1,0:T(8,128)}, u32[]{:S(2)}) copy-start(f32[1,128,1024]{2,1,0:T(8,128)} %copy.125) | copy-start | bytes 1572868
  250.1 190.1 %reduce-scatter.5.cloned.1.call-start = ((), (), s32[]{:S(2)}) async-start(), calls=%async_computation.8 | async-start | bytes 11796480 | tf_op jit(solution)/shard_map/reduce_scatter | solution.py:159
  270.9 6.5 copy-start.61
  270.9 7.2 %copy-start.59 = (f32[4,128]{1,0:T(4,128)S(1)}, f32[4,128]{1,0:T(4,128)}, u32[]{:S(2)}) copy-start(f32[4,128]{1,0:T(4,128)} %copy-done.58) | copy-start | bytes 6148
  270.9 296.3 %all-reduce.7.cloned.1.call-start = ((), (), s32[]{:S(2)}) async-start(), calls=%async_computation.10 | async-start | bytes 6291456 | tf_op jit(solution)/shard_map/psum | solution.py:255
  339.5 9.3 %copy-start.4 = (bf16[4,128,1024]{2,1,0:T(8,128)(2,1)S(1)}, bf16[4,128,1024]{2,1,0:T(8,128)(2,1)}, u32[]{:S(2)}) copy-start(bf16[4,128,1024]{2,1,0:T(8,128)(2,1)} %get-tuple-element.105) | copy-start | bytes 3145732
  372.0 6.2 copy-start.39
  388.6 51.7 %copy-start.38 = (f32[128,4,1]{1,2,0:T(1,128)S(1)}, f32[128,4,1]{1,2,0:T(1,128)}, u32[]{:S(2)}) copy-start(f32[128,4,1]{1,2,0:T(1,128)} %copy.157) | copy-start | bytes 6148
  464.1 7.0 copy-start.91
  464.1 7.0 copy-start.93
  464.1 7.0 copy-start.90
  464.1 7.0 copy-start.92
  464.1 7.0 copy-start.7
  464.1 7.0 copy-start.12
  464.1 7.0 copy-start.14
  464.1 91.9 %all-to-all-start.1 = ((bf16[10,1024,128]{2,0,1:T(8,128)(2,1)}), bf16[10,1024,128]{2,0,1:T(8,128)(2,1)}, u32[]{:S(2)}, u32[]{:S(2)}) async-start(bf16[10,1024,128]{2,0,1:T(8,128)(2,1)} %copy.129), calls=%async_computation.1 | async-start | bytes 8388608 | tf_op jit(solution)/shard_map/all_to_all | solution.py:253
  469.0 227.3 %all-reduce.5.cloned.1.call-start = ((), (), s32[]{:S(2)}) async-start(), calls=%async_computation.7 | async-start | bytes 327680 | tf_op jit(solution)/shard_map/psum | solution.py:260
  (78 other events, 256.0 us)
Sparse Core Ops, SparseCore 0:
  9.9 33.7 all-gather.5
  45.6 105.6 all-gather.3
  153.2 55.8 all-gather.7
  250.2 104.6 reduce-scatter.6
  358.2 81.9 reduce-scatter.4
  442.5 120.2 all-reduce.6
  568.9 127.3 all-reduce.4
where the time goes:
time: 712 us; the launch traced here: 705 us
  waiting for transfers between devices  289 us (41%)
  matrix products  148 us (21%)
  local copies, waits for them, and re-layouts  115 us (16%)
  blocking collectives  81.4 us (11%)
  other arithmetic  46.1 us (6%)
  between operations  15.9 us (2%)
  starting transfers between devices  9.98 us (1%)
    psum x1, waiting for transfers between devices, per_device(): lax.psum((gen_gain_grad, gen_in_grad, gen_out_grad, gen_bias_grad, norm_g...  121 us
    psum x1, blocking collectives, per_device(): lax.psum((gen_gain_grad, gen_in_grad, gen_out_grad, gen_bias_grad, norm_g...  81.4 us
    all_to_all x1, waiting for transfers between devices, per_device(): lax.all_to_all(stacked, 'seq', split_axis=2, concat_axis=1, tiled=True)  64.4 us
    reduce_scatter x1, waiting for transfers between devices, per_device(): lax.psum_scatter(jnp.concatenate([term_out, term_down], axis=1).astype(jn...  51.7 us
    unnamed x218, local copies, waits for them, and re-layouts  50.6 us
    dot_general x9, matrix products, per_device(): jnp.einsum('std,td->ts', grad_streams, hist_local[state].astype(jnp.float...  44.5 us
    dot_general x9, matrix products, per_device(): jnp.einsum('ts,std->td', mixing[:, :, state], grad_streams, precision=hig...  40.6 us
    all_gather x1, waiting for transfers between devices, per_device(): piece = lax.all_gather(w_in, 'seq', axis=0, tiled=True)  33.5 us
  transfers between devices with their start and end apart: 9, of which 5 were waited for; matrix products, arithmetic and copies ran while one was open for 36% of the time, Pallas kernels for 0%

commit v1 on v0

--- a/solution.py
+++ b/solution.py
@@ -80,7 +80,10 @@
 ):
     states = history.shape[0]
     stacked = jnp.concatenate([history, cotangent[None]], axis=0)
-    arrived = lax.all_to_all(stacked, "seq", split_axis=2, concat_axis=1, tiled=True)
+    arrived = jnp.concatenate(
+        lax.all_to_all(jnp.stack(jnp.split(stacked, lax.axis_size("seq"), axis=2)), "seq", 0, 0),
+        axis=1,
+    )
     arrived_rows = jnp.swapaxes(arrived, 1, 2)
     hist_local = arrived_rows[:states]
     cot_local = arrived_rows[states]

time: 712 us -> 699 us (0.982)
  local copies, waits for them, and re-layouts: 115 us -> 105 us
    all_to_all x1, waiting for transfers between devices: 64.4 us -> 34.3 us  [per_device(): lax.all_to_all(jnp.stack(jnp.split(stacked, lax.axis_size('seq'), axis=2)...]
    all_gather x1, waiting for transfers between devices: 33.5 us -> 56.2 us  [per_device(): piece = lax.all_gather(w_in, 'seq', axis=0, tiled=True)]
    all_to_all x2 -> x0, local copies, waits for them, and re-layouts: 9.41 us -> none  [per_device(): lax.all_to_all(stacked, 'seq', split_axis=2, concat_axis=1, tiled=True)]
    reshape x0 -> x2, local copies, waits for them, and re-layouts: none -> 7.21 us  [per_device(): jnp.concatenate(lax.all_to_all(jnp.stack(jnp.split(stacked, lax.axis_size...]
    unnamed x218 -> x217, local copies, waits for them, and re-layouts: 50.6 us -> 44.1 us
where the time goes in v1:
time: 699 us; the launch traced here: 687 us
  waiting for transfers between devices  282 us (40%)
  matrix products  148 us (21%)
  local copies, waits for them, and re-layouts  105 us (15%)
  blocking collectives  81.4 us (12%)
  other arithmetic  46.4 us (7%)
  between operations  15.9 us (2%)
  starting transfers between devices  9.16 us (1%)
    psum x1, waiting for transfers between devices, per_device(): lax.psum((gen_gain_grad, gen_in_grad, gen_out_grad, gen_bias_grad, norm_g...  121 us
    psum x1, blocking collectives, per_device(): lax.psum((gen_gain_grad, gen_in_grad, gen_out_grad, gen_bias_grad, norm_g...  81.4 us
    all_gather x1, waiting for transfers between devices, per_device(): piece = lax.all_gather(w_in, 'seq', axis=0, tiled=True)  56.2 us
    reduce_scatter x1, waiting for transfers between devices, per_device(): lax.psum_scatter(jnp.concatenate([term_out, term_down], axis=1).astype(jn...  51.6 us
    dot_general x9, matrix products, per_device(): jnp.einsum('std,td->ts', grad_streams, hist_local[state].astype(jnp.float...  44.5 us
    unnamed x217, local copies, waits for them, and re-layouts  44.1 us
    dot_general x9, matrix products, per_device(): jnp.einsum('ts,std->td', mixing[:, :, state], grad_streams, precision=hig...  40.6 us
    all_to_all x1, waiting for transfers between devices, per_device(): lax.all_to_all(jnp.stack(jnp.split(stacked, lax.axis_size('seq'), axis=2)...  34.3 us
  transfers between devices with their start and end apart: 9, of which 5 were waited for; matrix products, arithmetic and copies ran while one was open for 36% of the time, Pallas kernels for 0%

profile of v1, /device:TPU:8, one launch (start us, length us, event | category | flops | bytes accessed | tf_op | source)
XLA Modules:
  0.0 687.3 jit_solution(905097735796283608)
XLA Ops:
  25.0 34.3 %all-to-all-done = bf16[8,10,128,128]{3,2,1,0:T(8,128)(2,1)S(1)} async-done(((bf16[8,10,128,128]{3,2,1,0:T(8,128)(2,1)}), bf16[8,10,128,128]{3,2,1,0:T(8,128)(2,1)S(1)}, u32[]{:S(2)}, u32[]{:S(2)}) %all-to-all-start) | async-done | bytes 2621472 | tf_op jit(solution)/shard_map/all_to_all | solution.py:84
  77.3 56.2 %all-gather.4.cloned.1.call-done = bf16[1024,7,1024]{2,0,1:T(8,128)(2,1)} async-done(((bf16[128,7,1024]{2,0,1:T(8,128)(2,1)}), bf16[1024,7,1024]{2,0,1:T(8,128)(2,1)}) %all-gather.4.cloned.1.call-update) | async-done | bytes 14680080 | tf_op jit(solution)/shard_map/all_gather | solution.py:110
  133.5 5.0 fusion.6
  138.5 6.3 fusion.22
  167.1 7.2 %multiply_convert_fusion = (bf16[4,128,1024]{2,1,0:T(8,128)(2,1)}, f32[4,128,1024]{2,1,0:T(8,128)}) fusion(f32[7,128,1024]{2,1,0:T(8,128)} %copy-done.5), kind=kLoop, calls=%fused_computation.35 | loop fusion | flops 34078720 | bytes 5242880 | tf_op jit(solution)/shard_map/convert_element_type | solution.py:139
  174.3 17.0 %all-gather.8.cloned.1.call-done = bf16[1024,4096]{0,1:T(8,128)(2,1)} async-done(((bf16[128,4096]{0,1:T(8,128)(2,1)}), bf16[1024,4096]{0,1:T(8,128)(2,1)}) %all-gather.8.cloned.1.call-update) | async-done | bytes 8388624 | tf_op jit(solution)/shard_map/all_gather | solution.py:141
  191.3 8.0 %fusion.15 = f32[4,128,1024]{2,1,0:T(8,128)S(1)} fusion(f32[4,128,1024]{2,1,0:T(8,128)} %get-tuple-element.91, f32[7,128,1024]{2,1,0:T(8,128)} %copy-done.5, bf16[1024,4,1024]{0,2,1:T(8,128)(2,1)} %bitcast.397, pred[128]{0:T(512)(128)(4,1)S(1)} %copy-done.57, bf16[10,128,1024]{2,1,0:T(8,128)(2,1)} %bitcast.380), kind=kOutput, calls=%fused_computation.33 | convolution fusion | flops 1080688640 | bytes 14942336 | tf_op jit(solution)/shard_map/tn,njk->jtk/dot_general | solution.py:153
  205.5 8.3 %pad_maximum_fusion = bf16[1024,7,1024]{0,2,1:T(8,128)(2,1)} fusion(bf16[1024,4,1024]{0,2,1:T(8,128)(2,1)S(1)} %convert_bitcast_fusion, bf16[1024,3,1024]{0,2,1:T(8,128)(2,1)S(1)} %convert_bitcast_fusion.1), kind=kLoop, calls=%fused_computation | loop fusion | flops 7340032 | bytes 29360128 | tf_op jit(solution)/shard_map/concatenate | solution.py:212
  213.8 18.5 %copy.156 = bf16[1024,7168]{1,0:T(8,128)(2,1)} copy(bf16[1024,7168]{0,1:T(8,128)(2,1)} %bitcast.375) | data formatting | bytes 29360128
  246.8 6.3 pad_maximum_fusion.1
  260.3 5.9 multiply_reduce_fusion.5
  266.2 5.0 multiply_reduce_fusion.1
  273.7 4.8 fusion.68
  278.5 4.8 fusion.66
  283.4 5.0 fusion.64
  288.5 4.8 fusion.62
  293.9 4.8 fusion.60
  299.4 5.2 fusion.58
  305.3 4.8 fusion.56
  310.7 4.8 fusion.54
  316.1 5.6 fusion.52
  325.7 5.2 fusion.163
  331.0 4.9 convolution_bitcast_fusion.1
  344.6 4.4 fusion.159
  355.0 4.6 fusion.155
  370.8 51.6 %reduce-scatter.5.cloned.1.call-done = bf16[128,5120]{1,0:T(8,128)(2,1)} async-done(((bf16[1024,5120]{1,0:T(8,128)(2,1)}), bf16[128,5120]{1,0:T(8,128)(2,1)}) %reduce-scatter.5.cloned.1.call-update) | async-done | bytes 1310736 | tf_op jit(solution)/shard_map/reduce_scatter | solution.py:162
  422.5 4.4 fusion.151
  432.8 4.6 fusion.147
  439.4 6.8 copy.99
  446.3 4.8 all-to-all-start.1
  454.9 81.4 %all-reduce = (f32[4,9]{1,0:T(4,128)S(1)}, f32[]{:T(128)}, f32[4,9]{1,0:T(4,128)S(1)}, f32[1024]{0:T(1024)}, f32[40,4,9]{0,2,1:T(8,128)S(1)}, /*index=5*/f32[4,9...) all-reduce(f32[4,9]{1,0:T(4,128)S(1)} %copy-done.85, ...), channel_id=1, replica_groups=mesh['seq'=8,'dp'=4] {'seq','dp'}, use_global_device_ids=true, to_apply=%region_12.13 | all-reduce | flops 14861 | bytes 118888 | tf_op jit(solution)/shard_map/psum | solution.py:263
  556.9 121.5 %all-reduce.5.cloned.1.call-done = f32[1024,40]{0,1:T(8,128)} async-done(((f32[1024,40]{0,1:T(8,128)}), f32[1024,40]{0,1:T(8,128)}) %all-reduce.5.cloned.1.call-update) | async-done | bytes 163856 | tf_op jit(solution)/shard_map/psum | solution.py:263
  (350 shorter events, 155.0 us)
Async XLA Ops:
  7.2 60.7 %copy-start = (bf16[1024,40]{0,1:T(8,128)(2,1)S(1)}, bf16[1024,40]{0,1:T(8,128)(2,1)}, u32[]{:S(2)}) copy-start(bf16[1024,40]{0,1:T(8,128)(2,1)} %param.20) | copy-start | bytes 245764
  7.2 67.7 %all-gather.6.cloned.1.call-start = ((), (), s32[]{:S(2)}) async-start(), calls=%async_computation.5 | async-start | bytes 2359296 | tf_op jit(solution)/shard_map/all_gather | solution.py:141
  7.9 125.5 %all-gather.4.cloned.1.call-start = ((), (), s32[]{:S(2)}) async-start(), calls=%async_computation.4 | async-start | bytes 16515072 | tf_op jit(solution)/shard_map/all_gather | solution.py:110
  8.7 182.6 %all-gather.8.cloned.1.call-start = ((), (), s32[]{:S(2)}) async-start(), calls=%async_computation.6 | async-start | bytes 9437184 | tf_op jit(solution)/shard_map/all_gather | solution.py:141
  17.6 7.3 %copy-start.86 = (f32[2,1024]{1,0:T(2,128)S(1)}, f32[2,1024]{1,0:T(2,128)}, u32[]{:S(2)}) copy-start(f32[2,1024]{1,0:T(2,128)} %param.24) | copy-start | bytes 24580
  17.6 7.3 %copy-start.87 = (f32[2,1024]{1,0:T(2,128)S(1)}, f32[2,1024]{1,0:T(2,128)}, u32[]{:S(2)}) copy-start(f32[2,1024]{1,0:T(2,128)} %param.23) | copy-start | bytes 24580
  17.6 41.7 %all-to-all-start = ((bf16[8,10,128,128]{3,2,1,0:T(8,128)(2,1)}), bf16[8,10,128,128]{3,2,1,0:T(8,128)(2,1)S(1)}, u32[]{:S(2)}, u32[]{:S(2)}) async-start(bf16[8,10,128,128]{3,2,1,0:T(8,128)(2,1)} %fusion.82), calls=%async_computation | async-start | bytes 5242880 | tf_op jit(solution)/shard_map/all_to_all | solution.py:84
  21.4 345.4 %reduce-scatter.7.cloned.1.call-start = ((), (), s32[]{:S(2)}) async-start(), calls=%async_computation.9 | async-start | bytes 16515072
  24.0 50.9 %copy-start.56 = (pred[128]{0:T(512)(128)(4,1)}, pred[128]{0:T(512)(128)(4,1)S(1)}, u32[]{:S(2)}) copy-start(pred[128]{0:T(512)(128)(4,1)S(1)} %get-tuple-element.89) | copy-start | bytes 388
  24.8 108.7 %copy-start.78 = (f32[1,1024]{1,0:T(1,128)}, f32[1,1024]{1,0:T(1,128)S(1)}, u32[]{:S(2)}) copy-start(f32[1,1024]{1,0:T(1,128)S(1)} %get-tuple-element.137) | copy-start | bytes 12292
  24.8 113.6 %copy-start.82 = (f32[1,1024]{1,0:T(1,128)}, f32[1,1024]{1,0:T(1,128)S(1)}, u32[]{:S(2)}) copy-start(f32[1,1024]{1,0:T(1,128)S(1)} %get-tuple-element.138) | copy-start | bytes 12292
  138.5 6.3 copy-start.53
  167.1 24.2 %copy-start.57 = (pred[128]{0:T(512)(128)(4,1)S(1)}, pred[128]{0:T(512)(128)(4,1)}, u32[]{:S(2)}) copy-start(pred[128]{0:T(512)(128)(4,1)} %copy-done.56) | copy-start | bytes 388
  191.3 9.3 %copy-start.13 = (f32[1,128,1024]{2,1,0:T(8,128)S(1)}, f32[1,128,1024]{2,1,0:T(8,128)}, u32[]{:S(2)}) copy-start(f32[1,128,1024]{2,1,0:T(8,128)} %copy.97) | copy-start | bytes 1572868
  191.3 9.3 %copy-start.15 = (f32[1,128,1024]{2,1,0:T(8,128)S(1)}, f32[1,128,1024]{2,1,0:T(8,128)}, u32[]{:S(2)}) copy-start(f32[1,128,1024]{2,1,0:T(8,128)} %copy.96) | copy-start | bytes 1572868
  191.3 9.3 %copy-start.17 = (f32[1,128,1024]{2,1,0:T(8,128)S(1)}, f32[1,128,1024]{2,1,0:T(8,128)}, u32[]{:S(2)}) copy-start(f32[1,128,1024]{2,1,0:T(8,128)} %copy.95) | copy-start | bytes 1572868
  232.3 190.1 %reduce-scatter.5.cloned.1.call-start = ((), (), s32[]{:S(2)}) async-start(), calls=%async_computation.8 | async-start | bytes 11796480 | tf_op jit(solution)/shard_map/reduce_scatter | solution.py:162
  253.1 6.5 copy-start.61
  253.1 7.2 %copy-start.59 = (f32[4,128]{1,0:T(4,128)S(1)}, f32[4,128]{1,0:T(4,128)}, u32[]{:S(2)}) copy-start(f32[4,128]{1,0:T(4,128)} %copy-done.58) | copy-start | bytes 6148
  253.1 296.2 %all-reduce.7.cloned.1.call-start = ((), (), s32[]{:S(2)}) async-start(), calls=%async_computation.10 | async-start | bytes 6291456 | tf_op jit(solution)/shard_map/psum | solution.py:258
  321.7 9.3 %copy-start.6 = (bf16[4,128,1024]{2,1,0:T(8,128)(2,1)S(1)}, bf16[4,128,1024]{2,1,0:T(8,128)(2,1)}, u32[]{:S(2)}) copy-start(bf16[4,128,1024]{2,1,0:T(8,128)(2,1)} %get-tuple-element.90) | copy-start | bytes 3145732
  354.2 6.2 copy-start.39
  370.8 51.7 %copy-start.38 = (f32[128,4,1]{1,2,0:T(1,128)S(1)}, f32[128,4,1]{1,2,0:T(1,128)}, u32[]{:S(2)}) copy-start(f32[128,4,1]{1,2,0:T(1,128)} %copy.127) | copy-start | bytes 6148
  446.2 7.0 %copy-start.91 = (f32[1024]{0:T(1024)S(1)}, f32[1024]{0:T(1024)}, u32[]{:S(2)}) copy-start(f32[1024]{0:T(1024)} %get-tuple-element.66) | copy-start | bytes 12292
  446.2 7.0 %copy-start.93 = (f32[1024]{0:T(1024)S(1)}, f32[1024]{0:T(1024)}, u32[]{:S(2)}) copy-start(f32[1024]{0:T(1024)} %get-tuple-element.60) | copy-start | bytes 12292
  446.2 7.0 %copy-start.90 = (f32[1024]{0:T(1024)S(1)}, f32[1024]{0:T(1024)}, u32[]{:S(2)}) copy-start(f32[1024]{0:T(1024)} %get-tuple-element.71) | copy-start | bytes 12292
  446.2 7.0 %copy-start.92 = (f32[1024]{0:T(1024)S(1)}, f32[1024]{0:T(1024)}, u32[]{:S(2)}) copy-start(f32[1024]{0:T(1024)} %get-tuple-element.69) | copy-start | bytes 12292
  446.2 7.0 %copy-start.9 = (f32[4,128,1024]{2,1,0:T(8,128)S(1)}, f32[4,128,1024]{2,1,0:T(8,128)}, u32[]{:S(2)}) copy-start(f32[4,128,1024]{2,1,0:T(8,128)} %copy-done.8) | copy-start | bytes 6291460
  446.2 7.0 %copy-start.14 = (f32[1,128,1024]{2,1,0:T(8,128)S(1)}, f32[1,128,1024]{2,1,0:T(8,128)}, u32[]{:S(2)}) copy-start(f32[1,128,1024]{2,1,0:T(8,128)} %copy.97) | copy-start | bytes 1572868
  446.2 7.0 %copy-start.16 = (f32[1,128,1024]{2,1,0:T(8,128)S(1)}, f32[1,128,1024]{2,1,0:T(8,128)}, u32[]{:S(2)}) copy-start(f32[1,128,1024]{2,1,0:T(8,128)} %copy.96) | copy-start | bytes 1572868
  446.3 91.9 %all-to-all-start.1 = ((bf16[10,1024,128]{2,0,1:T(8,128)(2,1)}), bf16[10,1024,128]{2,0,1:T(8,128)(2,1)}, u32[]{:S(2)}, u32[]{:S(2)}) async-start(bf16[10,1024,128]{2,0,1:T(8,128)(2,1)} %copy.99), calls=%async_computation.1 | async-start | bytes 8388608 | tf_op jit(solution)/shard_map/all_to_all | solution.py:256
  451.1 227.3 %all-reduce.5.cloned.1.call-start = ((), (), s32[]{:S(2)}) async-start(), calls=%async_computation.7 | async-start | bytes 327680 | tf_op jit(solution)/shard_map/psum | solution.py:263
  (78 other events, 256.1 us)
Sparse Core Ops, SparseCore 0:
  9.9 41.6 all-gather.5
  53.5 79.9 all-gather.3
  135.4 55.8 all-gather.7
  232.4 104.6 reduce-scatter.6
  340.4 81.9 reduce-scatter.4
  424.7 120.2 all-reduce.6
  551.1 127.2 all-reduce.4
